TPU v7x, 256 devices: a whole 4x4x8 slice. The times are simulated.
256 devices in a mesh: section: 8 (over y, core), dp: 32 (over x, z).
Axes of the slice: x: 4, y: 4, z: 8, core: 2. Of those that a mesh axis runs over, the one named last changes fastest.
Arguments:
- tokens: bfloat16 [4, 1024, 2048], P(None, 'dp'), may hold values from -6 to 6
- norm_gain: bfloat16 [8, 2048], P('section'), may hold values from 0.25 to 1.75
- router_weight: bfloat16 [8, 2048, 32], P('section'), may hold values from -0.125 to 0.125
- gate_weight: bfloat16 [8, 32, 2048, 768], P('section', 'dp'), may hold values from -0.125 to 0.125
- up_weight: bfloat16 [8, 32, 2048, 768], P('section', 'dp'), may hold values from -0.125 to 0.125
- down_weight: bfloat16 [8, 32, 768, 2048], P('section', 'dp'), may hold values from -0.21875 to 0.21875
- routing: int32 [8, 4, 1024, 6], P('section', None, 'dp'), may hold values from 0 to 31, all different within a row; in each aligned block of 32 rows (0 to 31, 32 to 63, ..., all dimensions but the last counted through in order) at most 7 rows name the same one
Outputs:
- layer_outputs: bfloat16 [8, 4, 1024, 2048], P('section', None, 'dp')
- router_grad: float32 [8, 2048, 32], P('section', 'dp')
Inputs may be any that keep to these rules, and one draw needn't show every extreme that they name: `routing`: each token names 6 different experts. Among one index of dp's 32 tokens of one micro-batch and layer, at most 7 name the same expert, and in some of these blocks exactly 7 do.
All inputs are finite; a program needn't handle non-finite values.
Results may differ from a plain program's by a relative error of at most 0.019.
Values may be sent and summed in bfloat16 or wider, within the bound.
A program may use at most 64 MiB of HBM per device.

v0:
```python
import jax
import jax.numpy as jnp
from jax import lax
from jax.sharding import Mesh
from jax.sharding import PartitionSpec as P

DP = ("dp_0", "dp_1")
EPSILON = 1e-06


def over_axes(shard, axes):
    for axis in axes:
        shard = lax.psum(shard, axis)
    return shard


def from_behind(value, axis, steps):
    count = lax.axis_size(axis)
    initial, last = (max(0, -steps), min(count, count - steps))
    return lax.ppermute(value, axis, [(source, source + steps) for source in range(initial, last)])


def cut_along(shard, dim, peers):
    shape = shard.shape
    pieces = shard.reshape(*shape[:dim], peers, shape[dim] // peers, *shape[dim + 1 :])
    return jnp.moveaxis(pieces, dim, 0)


def summed_on_arrival(shard, axis, dim):
    pieces = cut_along(shard, dim, lax.axis_size(axis))
    arrived = lax.all_to_all(pieces, axis, split_axis=0, concat_axis=0, tiled=True)
    return arrived.astype(jnp.float32).sum(axis=0)


def normalize(states, gain):
    values = states.astype(jnp.float32)
    mean_square = jnp.mean(values * values, axis=-1, keepdims=True)
    return (values * lax.rsqrt(mean_square + EPSILON) * gain.astype(jnp.float32)).astype(
        jnp.bfloat16
    )


def expert_ffn(rows, w_gate, w_up, w_down):
    gated = jnp.dot(rows, w_gate, preferred_element_type=jnp.float32)
    upward = jnp.dot(rows, w_up, preferred_element_type=jnp.float32)
    hidden = (jax.nn.silu(gated) * upward).astype(jnp.bfloat16)
    return jnp.dot(hidden, w_down, preferred_element_type=jnp.float32).astype(jnp.bfloat16)


def slope_of(probs, share):
    return probs * (share - jnp.sum(probs * share, axis=-1, keepdims=True))


def outer_rows(normed_rows, slope_rows):
    return lax.dot_general(
        normed_rows.astype(jnp.float32),
        slope_rows,
        (((0,), (0,)), ((), ())),
        precision=lax.Precision.HIGHEST,
    )


def place(stack, index, value, active):
    previous = lax.dynamic_index_in_dim(stack, index, 0, keepdims=False)
    return lax.dynamic_update_index_in_dim(stack, jnp.where(active, value, previous), index, 0)


def on_device(tokens, norm_gain, router_weight, gate_weight, up_weight, down_weight, routing):
    sections = lax.axis_size("section")
    replicas = lax.axis_size(DP)
    position = lax.axis_index("section")
    micro = tokens.shape[0]
    rows = tokens.shape[1]
    width = tokens.shape[2]
    experts = router_weight.shape[2]
    chosen_count = routing.shape[3]
    slots = min(rows, rows * chosen_count // experts + 1)
    total_rows = micro * rows * replicas
    gain = norm_gain[0]
    w_router = router_weight[0]
    w_gate = gate_weight[0, 0]
    w_up = up_weight[0, 0]
    w_down = down_weight[0, 0]
    expert_ids = jnp.arange(experts, dtype=jnp.int32)
    hot_all = (routing[0][..., None] == expert_ids).astype(jnp.int32).sum(axis=2)
    local_counts = jnp.sum(hot_all, axis=(0, 1))
    slot_ids = jnp.arange(slots, dtype=jnp.int32)
    row_ids = jnp.arange(rows, dtype=jnp.int32)
    before = (row_ids[:, None] > row_ids[None, :]).astype(jnp.bfloat16)

    def section_work(states, hot, active):
        normed = normalize(states, gain)
        logits = jnp.dot(normed, w_router, preferred_element_type=jnp.float32)
        exps = jnp.exp(logits)
        probs = exps / jnp.sum(exps, axis=-1, keepdims=True)
        rank = jnp.dot(before, hot.astype(jnp.bfloat16), preferred_element_type=jnp.float32).astype(
            jnp.int32
        )
        match = ((hot.T[:, None, :] == 1) & (rank.T[:, None, :] == slot_ids[None, :, None])).astype(
            jnp.bfloat16
        )
        sent = jnp.einsum("ect,td->ecd", match, normed, preferred_element_type=jnp.float32).astype(
            jnp.bfloat16
        )

        def compute(flat):
            return expert_ffn(flat, w_gate, w_up, w_down)

        def skipped(flat):
            return jnp.zeros((flat.shape[0], width), jnp.bfloat16)

        received = lax.all_to_all(sent, DP, split_axis=0, concat_axis=0, tiled=True)
        flat = received.reshape(-1, width)
        produced = lax.cond(active, compute, skipped, flat)
        returned = lax.all_to_all(
            produced.reshape(received.shape), DP, split_axis=0, concat_axis=0, tiled=True
        )
        chosen = hot.astype(jnp.float32) * probs
        weights = (chosen / jnp.sum(chosen, axis=-1, keepdims=True)).astype(jnp.bfloat16)
        combine = match * weights.T[:, None, :]
        mixed = jnp.einsum("ect,ecd->td", combine, returned, preferred_element_type=jnp.float32)
        result = (states.astype(jnp.float32) + mixed).astype(jnp.bfloat16)
        return (result, normed, probs)

    def advance(step, incoming):
        index = step - position
        active = (index >= 0) & (index < micro)
        clipped = jnp.clip(index, 0, micro - 1)
        first = lax.dynamic_index_in_dim(tokens, jnp.minimum(step, micro - 1), 0, keepdims=False)
        states = jnp.where(position == 0, first, incoming)
        hot = lax.dynamic_index_in_dim(hot_all, clipped, 0, keepdims=False)
        result, normed, probs = section_work(states, hot, active)
        passed = from_behind(result, "section", 1)
        return (active, clipped, result, normed, probs, passed)

    steps = micro + sections - 1
    incoming = jnp.zeros((rows, width), jnp.bfloat16)
    outputs = jnp.zeros((micro, rows, width), jnp.bfloat16)
    counts = over_axes(local_counts, DP)
    share = experts * counts.astype(jnp.float32) / (chosen_count * total_rows)

    def loop_before(step, carry):
        received, stored, gradient = carry
        active, clipped, result, normed, probs, passed = advance(step, received)
        contribution = outer_rows(normed, slope_of(probs, share))
        gradient = gradient + jnp.where(active, contribution, jnp.zeros_like(contribution))
        return (passed, place(stored, clipped, result, active), gradient)

    start_carry = (incoming, outputs, jnp.zeros((width, experts), jnp.float32))
    final = lax.fori_loop(0, steps, loop_before, start_carry)
    outputs = final[1]
    grad_rows = summed_on_arrival(final[2].astype(jnp.bfloat16), DP, 0)
    return (outputs[None], grad_rows[None])


def solution(mesh):
    torus = Mesh(mesh.devices.reshape(mesh.shape["section"], 4, 8), ("section", "dp_0", "dp_1"))
    in_specs = (
        P(None, DP, None),
        P("section", None),
        P("section", None, None),
        P("section", DP, None, None),
        P("section", DP, None, None),
        P("section", DP, None, None),
        P("section", None, DP, None),
    )
    out_specs = (P("section", None, DP, None), P("section", DP, None))
    return jax.shard_map(
        on_device, mesh=torus, in_specs=in_specs, out_specs=out_specs, check_vma=False
    )
```

profile of v0, /device:TPU:8, one launch (start us, length us, event | category | flops | bytes accessed | tf_op | source)
XLA Modules:
  0.0 916.3 jit_solution(12094145917065917706)
XLA Ops:
  29.3 867.1 %while.19 = (s32[]{:T(128)}, bf16[32,2048]{1,0:T(8,128)(2,1)S(1)}, bf16[4,32,2048]{2,1,0:T(8,128)(2,1)}, f32[2048,32]{0,1:T(8,128)S(1)}, pred[]{:T(512)}, /*inde...) while((s32[]{:T(128)}, bf16[32,2048]{1,0:T(8,128)(2,1)S(1)}, ...), condition=%wide.region_11.12_spmd.clone, body=%wide.region_4.11_spmd.clone.sunk | while | flops 2205590528 | bytes 29810108 | solution.py:150
  37.0 23.3 %all-to-all-done = bf16[32,7,2048]{2,1,0:T(8,128)(2,1)S(1)} async-done(((bf16[32,7,2048]{2,1,0:T(8,128)(2,1)}), bf16[32,7,2048]{2,1,0:T(8,128)(2,1)S(1)}, u32[]{:S(2)}, u32[]{:S(2)}) %all-to-all-start) | async-done | bytes 917536 | tf_op jit(solution)/shard_map/while/body/eval_jaxpr/all_to_all | solution.py:112
  68.7 21.5 %all-to-all-done.1 = bf16[32,7,2048]{2,1,0:T(8,128)(2,1)S(1)} async-done(((bf16[32,7,2048]{2,1,0:T(8,128)(2,1)}), bf16[32,7,2048]{2,1,0:T(8,128)(2,1)S(1)}, u32[]{:S(2)}, u32[]{:S(2)}) %all-to-all-start.1) | async-done | bytes 917536 | tf_op jit(solution)/shard_map/while/body/eval_jaxpr/all_to_all | solution.py:115
  107.0 28.2 %all-to-all-done = bf16[32,7,2048]{2,1,0:T(8,128)(2,1)S(1)} async-done(((bf16[32,7,2048]{2,1,0:T(8,128)(2,1)}), bf16[32,7,2048]{2,1,0:T(8,128)(2,1)S(1)}, u32[]{:S(2)}, u32[]{:S(2)}) %all-to-all-start) | async-done | bytes 917536 | tf_op jit(solution)/shard_map/while/body/eval_jaxpr/all_to_all | solution.py:112
  143.0 26.8 %all-to-all-done.1 = bf16[32,7,2048]{2,1,0:T(8,128)(2,1)S(1)} async-done(((bf16[32,7,2048]{2,1,0:T(8,128)(2,1)}), bf16[32,7,2048]{2,1,0:T(8,128)(2,1)S(1)}, u32[]{:S(2)}, u32[]{:S(2)}) %all-to-all-start.1) | async-done | bytes 917536 | tf_op jit(solution)/shard_map/while/body/eval_jaxpr/all_to_all | solution.py:115
  193.8 20.4 %all-to-all-done = bf16[32,7,2048]{2,1,0:T(8,128)(2,1)S(1)} async-done(((bf16[32,7,2048]{2,1,0:T(8,128)(2,1)}), bf16[32,7,2048]{2,1,0:T(8,128)(2,1)S(1)}, u32[]{:S(2)}, u32[]{:S(2)}) %all-to-all-start) | async-done | bytes 917536 | tf_op jit(solution)/shard_map/while/body/eval_jaxpr/all_to_all | solution.py:112
  230.2 16.7 %all-to-all-done.1 = bf16[32,7,2048]{2,1,0:T(8,128)(2,1)S(1)} async-done(((bf16[32,7,2048]{2,1,0:T(8,128)(2,1)}), bf16[32,7,2048]{2,1,0:T(8,128)(2,1)S(1)}, u32[]{:S(2)}, u32[]{:S(2)}) %all-to-all-start.1) | async-done | bytes 917536 | tf_op jit(solution)/shard_map/while/body/eval_jaxpr/all_to_all | solution.py:115
  250.5 17.6 %collective-permute-done = bf16[32,2048]{1,0:T(8,128)(2,1)S(1)} collective-permute-done((bf16[32,2048]{1,0:T(8,128)(2,1)S(1)}, bf16[32,2048]{1,0:T(8,128)(2,1)S(1)}, u32[]{:S(2)}, u32[]{:S(2)}) %collective-permute-start) | collective-permute-done | bytes 131104 | tf_op jit(solution)/shard_map/while/body/eval_jaxpr/ppermute | solution.py:20
  279.9 18.1 %all-to-all-done = bf16[32,7,2048]{2,1,0:T(8,128)(2,1)S(1)} async-done(((bf16[32,7,2048]{2,1,0:T(8,128)(2,1)}), bf16[32,7,2048]{2,1,0:T(8,128)(2,1)S(1)}, u32[]{:S(2)}, u32[]{:S(2)}) %all-to-all-start) | async-done | bytes 917536 | tf_op jit(solution)/shard_map/while/body/eval_jaxpr/all_to_all | solution.py:112
  315.9 16.7 %all-to-all-done.1 = bf16[32,7,2048]{2,1,0:T(8,128)(2,1)S(1)} async-done(((bf16[32,7,2048]{2,1,0:T(8,128)(2,1)}), bf16[32,7,2048]{2,1,0:T(8,128)(2,1)S(1)}, u32[]{:S(2)}, u32[]{:S(2)}) %all-to-all-start.1) | async-done | bytes 917536 | tf_op jit(solution)/shard_map/while/body/eval_jaxpr/all_to_all | solution.py:115
  336.2 18.0 %collective-permute-done = bf16[32,2048]{1,0:T(8,128)(2,1)S(1)} collective-permute-done((bf16[32,2048]{1,0:T(8,128)(2,1)S(1)}, bf16[32,2048]{1,0:T(8,128)(2,1)S(1)}, u32[]{:S(2)}, u32[]{:S(2)}) %collective-permute-start) | collective-permute-done | bytes 131104 | tf_op jit(solution)/shard_map/while/body/eval_jaxpr/ppermute | solution.py:20
  365.9 18.1 %all-to-all-done = bf16[32,7,2048]{2,1,0:T(8,128)(2,1)S(1)} async-done(((bf16[32,7,2048]{2,1,0:T(8,128)(2,1)}), bf16[32,7,2048]{2,1,0:T(8,128)(2,1)S(1)}, u32[]{:S(2)}, u32[]{:S(2)}) %all-to-all-start) | async-done | bytes 917536 | tf_op jit(solution)/shard_map/while/body/eval_jaxpr/all_to_all | solution.py:112
  402.0 16.7 %all-to-all-done.1 = bf16[32,7,2048]{2,1,0:T(8,128)(2,1)S(1)} async-done(((bf16[32,7,2048]{2,1,0:T(8,128)(2,1)}), bf16[32,7,2048]{2,1,0:T(8,128)(2,1)S(1)}, u32[]{:S(2)}, u32[]{:S(2)}) %all-to-all-start.1) | async-done | bytes 917536 | tf_op jit(solution)/shard_map/while/body/eval_jaxpr/all_to_all | solution.py:115
  444.8 17.4 %all-to-all-done = bf16[32,7,2048]{2,1,0:T(8,128)(2,1)S(1)} async-done(((bf16[32,7,2048]{2,1,0:T(8,128)(2,1)}), bf16[32,7,2048]{2,1,0:T(8,128)(2,1)S(1)}, u32[]{:S(2)}, u32[]{:S(2)}) %all-to-all-start) | async-done | bytes 917536 | tf_op jit(solution)/shard_map/while/body/eval_jaxpr/all_to_all | solution.py:112
  480.4 16.7 %all-to-all-done.1 = bf16[32,7,2048]{2,1,0:T(8,128)(2,1)S(1)} async-done(((bf16[32,7,2048]{2,1,0:T(8,128)(2,1)}), bf16[32,7,2048]{2,1,0:T(8,128)(2,1)S(1)}, u32[]{:S(2)}, u32[]{:S(2)}) %all-to-all-start.1) | async-done | bytes 917536 | tf_op jit(solution)/shard_map/while/body/eval_jaxpr/all_to_all | solution.py:115
  522.1 17.8 %all-to-all-done = bf16[32,7,2048]{2,1,0:T(8,128)(2,1)S(1)} async-done(((bf16[32,7,2048]{2,1,0:T(8,128)(2,1)}), bf16[32,7,2048]{2,1,0:T(8,128)(2,1)S(1)}, u32[]{:S(2)}, u32[]{:S(2)}) %all-to-all-start) | async-done | bytes 917536 | tf_op jit(solution)/shard_map/while/body/eval_jaxpr/all_to_all | solution.py:112
  548.8 24.1 %all-to-all-done.1 = bf16[32,7,2048]{2,1,0:T(8,128)(2,1)S(1)} async-done(((bf16[32,7,2048]{2,1,0:T(8,128)(2,1)}), bf16[32,7,2048]{2,1,0:T(8,128)(2,1)S(1)}, u32[]{:S(2)}, u32[]{:S(2)}) %all-to-all-start.1) | async-done | bytes 917536 | tf_op jit(solution)/shard_map/while/body/eval_jaxpr/all_to_all | solution.py:115
  599.3 18.1 %all-to-all-done = bf16[32,7,2048]{2,1,0:T(8,128)(2,1)S(1)} async-done(((bf16[32,7,2048]{2,1,0:T(8,128)(2,1)}), bf16[32,7,2048]{2,1,0:T(8,128)(2,1)S(1)}, u32[]{:S(2)}, u32[]{:S(2)}) %all-to-all-start) | async-done | bytes 917536 | tf_op jit(solution)/shard_map/while/body/eval_jaxpr/all_to_all | solution.py:112
  628.7 16.7 %all-to-all-done.1 = bf16[32,7,2048]{2,1,0:T(8,128)(2,1)S(1)} async-done(((bf16[32,7,2048]{2,1,0:T(8,128)(2,1)}), bf16[32,7,2048]{2,1,0:T(8,128)(2,1)S(1)}, u32[]{:S(2)}, u32[]{:S(2)}) %all-to-all-start.1) | async-done | bytes 917536 | tf_op jit(solution)/shard_map/while/body/eval_jaxpr/all_to_all | solution.py:115
  676.5 20.5 %all-to-all-done = bf16[32,7,2048]{2,1,0:T(8,128)(2,1)S(1)} async-done(((bf16[32,7,2048]{2,1,0:T(8,128)(2,1)}), bf16[32,7,2048]{2,1,0:T(8,128)(2,1)S(1)}, u32[]{:S(2)}, u32[]{:S(2)}) %all-to-all-start) | async-done | bytes 917536 | tf_op jit(solution)/shard_map/while/body/eval_jaxpr/all_to_all | solution.py:112
  753.7 18.1 %all-to-all-done = bf16[32,7,2048]{2,1,0:T(8,128)(2,1)S(1)} async-done(((bf16[32,7,2048]{2,1,0:T(8,128)(2,1)}), bf16[32,7,2048]{2,1,0:T(8,128)(2,1)S(1)}, u32[]{:S(2)}, u32[]{:S(2)}) %all-to-all-start) | async-done | bytes 917536 | tf_op jit(solution)/shard_map/while/body/eval_jaxpr/all_to_all | solution.py:112
  782.9 16.7 %all-to-all-done.1 = bf16[32,7,2048]{2,1,0:T(8,128)(2,1)S(1)} async-done(((bf16[32,7,2048]{2,1,0:T(8,128)(2,1)}), bf16[32,7,2048]{2,1,0:T(8,128)(2,1)S(1)}, u32[]{:S(2)}, u32[]{:S(2)}) %all-to-all-start.1) | async-done | bytes 917536 | tf_op jit(solution)/shard_map/while/body/eval_jaxpr/all_to_all | solution.py:115
  831.0 20.9 %all-to-all-done = bf16[32,7,2048]{2,1,0:T(8,128)(2,1)S(1)} async-done(((bf16[32,7,2048]{2,1,0:T(8,128)(2,1)}), bf16[32,7,2048]{2,1,0:T(8,128)(2,1)S(1)}, u32[]{:S(2)}, u32[]{:S(2)}) %all-to-all-start) | async-done | bytes 917536 | tf_op jit(solution)/shard_map/while/body/eval_jaxpr/all_to_all | solution.py:112
  897.0 18.4 %all_to_all.29 = bf16[32,2,1024]{2,1,0:T(2,128)(2,1)S(1)} all-to-all(bf16[32,2,1024]{2,1,0:T(2,128)(2,1)S(1)} %reshape.60), channel_id=1, replica_groups=mesh['section'=8,'dp_0'=4,'dp_1'=8] {'dp_0','dp_1'}, dimensions={0} | all-to-all | bytes 262144 | tf_op jit(solution)/shard_map/all_to_all | solution.py:31
  (299 shorter events, 503.4 us)
Async XLA Ops:
  32.8 27.5 %all-to-all-start = ((bf16[32,7,2048]{2,1,0:T(8,128)(2,1)}), bf16[32,7,2048]{2,1,0:T(8,128)(2,1)S(1)}, u32[]{:S(2)}, u32[]{:S(2)}) async-start(bf16[32,7,2048]{2,1,0:T(8,128)(2,1)} %copy.69), calls=%async_computation | async-start | bytes 2097152 | tf_op jit(solution)/shard_map/while/body/eval_jaxpr/all_to_all | solution.py:112
  61.7 28.5 %all-to-all-start.1 = ((bf16[32,7,2048]{2,1,0:T(8,128)(2,1)}), bf16[32,7,2048]{2,1,0:T(8,128)(2,1)S(1)}, u32[]{:S(2)}, u32[]{:S(2)}) async-start(bf16[32,7,2048]{2,1,0:T(8,128)(2,1)} %reshape.63), calls=%async_computation.1 | async-start | bytes 2097152 | tf_op jit(solution)/shard_map/while/body/eval_jaxpr/all_to_all | solution.py:115
  101.3 33.9 %all-to-all-start = ((bf16[32,7,2048]{2,1,0:T(8,128)(2,1)}), bf16[32,7,2048]{2,1,0:T(8,128)(2,1)S(1)}, u32[]{:S(2)}, u32[]{:S(2)}) async-start(bf16[32,7,2048]{2,1,0:T(8,128)(2,1)} %copy.69), calls=%async_computation | async-start | bytes 2097152 | tf_op jit(solution)/shard_map/while/body/eval_jaxpr/all_to_all | solution.py:112
  136.6 33.2 %all-to-all-start.1 = ((bf16[32,7,2048]{2,1,0:T(8,128)(2,1)}), bf16[32,7,2048]{2,1,0:T(8,128)(2,1)S(1)}, u32[]{:S(2)}, u32[]{:S(2)}) async-start(bf16[32,7,2048]{2,1,0:T(8,128)(2,1)} %reshape.63), calls=%async_computation.1 | async-start | bytes 2097152 | tf_op jit(solution)/shard_map/while/body/eval_jaxpr/all_to_all | solution.py:115
  185.0 29.2 %all-to-all-start = ((bf16[32,7,2048]{2,1,0:T(8,128)(2,1)}), bf16[32,7,2048]{2,1,0:T(8,128)(2,1)S(1)}, u32[]{:S(2)}, u32[]{:S(2)}) async-start(bf16[32,7,2048]{2,1,0:T(8,128)(2,1)} %copy.69), calls=%async_computation | async-start | bytes 2097152 | tf_op jit(solution)/shard_map/while/body/eval_jaxpr/all_to_all | solution.py:112
  224.4 22.4 %all-to-all-start.1 = ((bf16[32,7,2048]{2,1,0:T(8,128)(2,1)}), bf16[32,7,2048]{2,1,0:T(8,128)(2,1)S(1)}, u32[]{:S(2)}, u32[]{:S(2)}) async-start(bf16[32,7,2048]{2,1,0:T(8,128)(2,1)} %reshape.63), calls=%async_computation.1 | async-start | bytes 2097152 | tf_op jit(solution)/shard_map/while/body/eval_jaxpr/all_to_all | solution.py:115
  248.2 19.9 %collective-permute-start = (bf16[32,2048]{1,0:T(8,128)(2,1)S(1)}, bf16[32,2048]{1,0:T(8,128)(2,1)S(1)}, u32[]{:S(2)}, u32[]{:S(2)}) collective-permute-start(bf16[32,2048]{1,0:T(8,128)(2,1)S(1)} %get-tuple-element.542), channel_id=1, source_target_pairs={{0,32},{32,64},{64,96},{96,128},{128,160},{160,192},{192,224},{1,3... | collective-permute-start | bytes 393224 | tf_op jit(solution)/shard_map/while/body/eval_jaxpr/ppermute | solution.py:20
  271.6 26.4 %all-to-all-start = ((bf16[32,7,2048]{2,1,0:T(8,128)(2,1)}), bf16[32,7,2048]{2,1,0:T(8,128)(2,1)S(1)}, u32[]{:S(2)}, u32[]{:S(2)}) async-start(bf16[32,7,2048]{2,1,0:T(8,128)(2,1)} %copy.69), calls=%async_computation | async-start | bytes 2097152 | tf_op jit(solution)/shard_map/while/body/eval_jaxpr/all_to_all | solution.py:112
  308.2 24.4 %all-to-all-start.1 = ((bf16[32,7,2048]{2,1,0:T(8,128)(2,1)}), bf16[32,7,2048]{2,1,0:T(8,128)(2,1)S(1)}, u32[]{:S(2)}, u32[]{:S(2)}) async-start(bf16[32,7,2048]{2,1,0:T(8,128)(2,1)} %reshape.63), calls=%async_computation.1 | async-start | bytes 2097152 | tf_op jit(solution)/shard_map/while/body/eval_jaxpr/all_to_all | solution.py:115
  334.0 20.2 %collective-permute-start = (bf16[32,2048]{1,0:T(8,128)(2,1)S(1)}, bf16[32,2048]{1,0:T(8,128)(2,1)S(1)}, u32[]{:S(2)}, u32[]{:S(2)}) collective-permute-start(bf16[32,2048]{1,0:T(8,128)(2,1)S(1)} %get-tuple-element.542), channel_id=1, source_target_pairs={{0,32},{32,64},{64,96},{96,128},{128,160},{160,192},{192,224},{1,3... | collective-permute-start | bytes 393224 | tf_op jit(solution)/shard_map/while/body/eval_jaxpr/ppermute | solution.py:20
  357.6 26.4 %all-to-all-start = ((bf16[32,7,2048]{2,1,0:T(8,128)(2,1)}), bf16[32,7,2048]{2,1,0:T(8,128)(2,1)S(1)}, u32[]{:S(2)}, u32[]{:S(2)}) async-start(bf16[32,7,2048]{2,1,0:T(8,128)(2,1)} %copy.69), calls=%async_computation | async-start | bytes 2097152 | tf_op jit(solution)/shard_map/while/body/eval_jaxpr/all_to_all | solution.py:112
  394.3 24.4 %all-to-all-start.1 = ((bf16[32,7,2048]{2,1,0:T(8,128)(2,1)}), bf16[32,7,2048]{2,1,0:T(8,128)(2,1)S(1)}, u32[]{:S(2)}, u32[]{:S(2)}) async-start(bf16[32,7,2048]{2,1,0:T(8,128)(2,1)} %reshape.63), calls=%async_computation.1 | async-start | bytes 2097152 | tf_op jit(solution)/shard_map/while/body/eval_jaxpr/all_to_all | solution.py:115
  438.9 23.4 %all-to-all-start = ((bf16[32,7,2048]{2,1,0:T(8,128)(2,1)}), bf16[32,7,2048]{2,1,0:T(8,128)(2,1)S(1)}, u32[]{:S(2)}, u32[]{:S(2)}) async-start(bf16[32,7,2048]{2,1,0:T(8,128)(2,1)} %copy.69), calls=%async_computation | async-start | bytes 2097152 | tf_op jit(solution)/shard_map/while/body/eval_jaxpr/all_to_all | solution.py:112
  472.5 24.6 %all-to-all-start.1 = ((bf16[32,7,2048]{2,1,0:T(8,128)(2,1)}), bf16[32,7,2048]{2,1,0:T(8,128)(2,1)S(1)}, u32[]{:S(2)}, u32[]{:S(2)}) async-start(bf16[32,7,2048]{2,1,0:T(8,128)(2,1)} %reshape.63), calls=%async_computation.1 | async-start | bytes 2097152 | tf_op jit(solution)/shard_map/while/body/eval_jaxpr/all_to_all | solution.py:115
  513.8 26.1 %all-to-all-start = ((bf16[32,7,2048]{2,1,0:T(8,128)(2,1)}), bf16[32,7,2048]{2,1,0:T(8,128)(2,1)S(1)}, u32[]{:S(2)}, u32[]{:S(2)}) async-start(bf16[32,7,2048]{2,1,0:T(8,128)(2,1)} %copy.69), calls=%async_computation | async-start | bytes 2097152 | tf_op jit(solution)/shard_map/while/body/eval_jaxpr/all_to_all | solution.py:112
  541.3 31.7 %all-to-all-start.1 = ((bf16[32,7,2048]{2,1,0:T(8,128)(2,1)}), bf16[32,7,2048]{2,1,0:T(8,128)(2,1)S(1)}, u32[]{:S(2)}, u32[]{:S(2)}) async-start(bf16[32,7,2048]{2,1,0:T(8,128)(2,1)} %reshape.63), calls=%async_computation.1 | async-start | bytes 2097152 | tf_op jit(solution)/shard_map/while/body/eval_jaxpr/all_to_all | solution.py:115
  591.0 26.4 %all-to-all-start = ((bf16[32,7,2048]{2,1,0:T(8,128)(2,1)}), bf16[32,7,2048]{2,1,0:T(8,128)(2,1)S(1)}, u32[]{:S(2)}, u32[]{:S(2)}) async-start(bf16[32,7,2048]{2,1,0:T(8,128)(2,1)} %copy.69), calls=%async_computation | async-start | bytes 2097152 | tf_op jit(solution)/shard_map/while/body/eval_jaxpr/all_to_all | solution.py:112
  618.8 26.5 %all-to-all-start.1 = ((bf16[32,7,2048]{2,1,0:T(8,128)(2,1)}), bf16[32,7,2048]{2,1,0:T(8,128)(2,1)S(1)}, u32[]{:S(2)}, u32[]{:S(2)}) async-start(bf16[32,7,2048]{2,1,0:T(8,128)(2,1)} %reshape.63), calls=%async_computation.1 | async-start | bytes 2097152 | tf_op jit(solution)/shard_map/while/body/eval_jaxpr/all_to_all | solution.py:115
  668.2 28.8 %all-to-all-start = ((bf16[32,7,2048]{2,1,0:T(8,128)(2,1)}), bf16[32,7,2048]{2,1,0:T(8,128)(2,1)S(1)}, u32[]{:S(2)}, u32[]{:S(2)}) async-start(bf16[32,7,2048]{2,1,0:T(8,128)(2,1)} %copy.69), calls=%async_computation | async-start | bytes 2097152 | tf_op jit(solution)/shard_map/while/body/eval_jaxpr/all_to_all | solution.py:112
  698.4 28.3 %all-to-all-start.1 = ((bf16[32,7,2048]{2,1,0:T(8,128)(2,1)}), bf16[32,7,2048]{2,1,0:T(8,128)(2,1)S(1)}, u32[]{:S(2)}, u32[]{:S(2)}) async-start(bf16[32,7,2048]{2,1,0:T(8,128)(2,1)} %reshape.63), calls=%async_computation.1 | async-start | bytes 2097152 | tf_op jit(solution)/shard_map/while/body/eval_jaxpr/all_to_all | solution.py:115
  745.4 26.4 %all-to-all-start = ((bf16[32,7,2048]{2,1,0:T(8,128)(2,1)}), bf16[32,7,2048]{2,1,0:T(8,128)(2,1)S(1)}, u32[]{:S(2)}, u32[]{:S(2)}) async-start(bf16[32,7,2048]{2,1,0:T(8,128)(2,1)} %copy.69), calls=%async_computation | async-start | bytes 2097152 | tf_op jit(solution)/shard_map/while/body/eval_jaxpr/all_to_all | solution.py:112
  773.2 26.3 %all-to-all-start.1 = ((bf16[32,7,2048]{2,1,0:T(8,128)(2,1)}), bf16[32,7,2048]{2,1,0:T(8,128)(2,1)S(1)}, u32[]{:S(2)}, u32[]{:S(2)}) async-start(bf16[32,7,2048]{2,1,0:T(8,128)(2,1)} %reshape.63), calls=%async_computation.1 | async-start | bytes 2097152 | tf_op jit(solution)/shard_map/while/body/eval_jaxpr/all_to_all | solution.py:115
  822.7 29.2 %all-to-all-start = ((bf16[32,7,2048]{2,1,0:T(8,128)(2,1)}), bf16[32,7,2048]{2,1,0:T(8,128)(2,1)S(1)}, u32[]{:S(2)}, u32[]{:S(2)}) async-start(bf16[32,7,2048]{2,1,0:T(8,128)(2,1)} %copy.69), calls=%async_computation | async-start | bytes 2097152 | tf_op jit(solution)/shard_map/while/body/eval_jaxpr/all_to_all | solution.py:112
  853.3 27.9 %all-to-all-start.1 = ((bf16[32,7,2048]{2,1,0:T(8,128)(2,1)}), bf16[32,7,2048]{2,1,0:T(8,128)(2,1)S(1)}, u32[]{:S(2)}, u32[]{:S(2)}) async-start(bf16[32,7,2048]{2,1,0:T(8,128)(2,1)} %reshape.63), calls=%async_computation.1 | async-start | bytes 2097152 | tf_op jit(solution)/shard_map/while/body/eval_jaxpr/all_to_all | solution.py:115
  (9 other events, 120.9 us)
where the time goes:
time: 920 us; the launch traced here: 916 us
  waiting for transfers between devices  563 us (61%)
  starting transfers between devices  180 us (20%)
  matrix products  63.6 us (7%)
  local copies, waits for them, and re-layouts  49.8 us (5%)
  blocking collectives  43.4 us (5%)
  other arithmetic  14.7 us (2%)
    all_to_all x11, waiting for transfers between devices, section_work(): received = lax.all_to_all(sent, DP, split_axis=0, concat_axis=0, tiled=True)  221 us
    all_to_all x11, waiting for transfers between devices, section_work(): lax.all_to_all(produced.reshape(received.shape), DP, split_axis=0, concat...  206 us
    ppermute x11, waiting for transfers between devices, from_behind(): lax.ppermute(value, axis, [(source, source + steps) for source in range(i...  136 us
    all_to_all x11, starting transfers between devices, section_work(): received = lax.all_to_all(sent, DP, split_axis=0, concat_axis=0, tiled=True)  82.5 us
    all_to_all x11, starting transfers between devices, section_work(): lax.all_to_all(produced.reshape(received.shape), DP, split_axis=0, concat...  76.3 us
    psum x2, blocking collectives, over_axes(): shard = lax.psum(shard, axis)  25 us
    ppermute x11, starting transfers between devices, from_behind(): lax.ppermute(value, axis, [(source, source + steps) for source in range(i...  21 us
    dot_general x4, matrix products, expert_ffn(): jnp.dot(hidden, w_down, preferred_element_type=jnp.float32)  19.9 us
  transfers between devices with their start and end apart: 33, of which 33 were waited for; matrix products, arithmetic and copies ran while one was open for 2% of the time, Pallas kernels for 0%

commit v1 on v0

--- a/solution.py
+++ b/solution.py
@@ -10,7 +10,7 @@
 
 def over_axes(shard, axes):
     for axis in axes:
-        shard = lax.psum(shard, axis)
+        shard = jnp.sum(lax.all_gather(shard, axis), axis=0)
     return shard
 
 

time: 920 us -> 924 us (level)
    psum x2 -> x0, blocking collectives: 25 us -> none  [over_axes(): shard = lax.psum(shard, axis)]
    unnamed x0 -> x2, blocking collectives: none -> 25 us
where the time goes in v1:
time: 924 us; the launch traced here: 921 us
  waiting for transfers between devices  563 us (61%)
  starting transfers between devices  180 us (19%)
  matrix products  63.5 us (7%)
  local copies, waits for them, and re-layouts  53 us (6%)
  blocking collectives  43.4 us (5%)
  other arithmetic  14.8 us (2%)
    all_to_all x11, waiting for transfers between devices, section_work(): received = lax.all_to_all(sent, DP, split_axis=0, concat_axis=0, tiled=True)  221 us
    all_to_all x11, waiting for transfers between devices, section_work(): lax.all_to_all(produced.reshape(received.shape), DP, split_axis=0, concat...  206 us
    ppermute x11, waiting for transfers between devices, from_behind(): lax.ppermute(value, axis, [(source, source + steps) for source in range(i...  136 us
    all_to_all x11, starting transfers between devices, section_work(): received = lax.all_to_all(sent, DP, split_axis=0, concat_axis=0, tiled=True)  82.5 us
    all_to_all x11, starting transfers between devices, section_work(): lax.all_to_all(produced.reshape(received.shape), DP, split_axis=0, concat...  76.1 us
    unnamed x2, blocking collectives  25 us
    ppermute x11, starting transfers between devices, from_behind(): lax.ppermute(value, axis, [(source, source + steps) for source in range(i...  21 us
    dot_general x4, matrix products, expert_ffn(): jnp.dot(hidden, w_down, preferred_element_type=jnp.float32)  19.9 us
  transfers between devices with their start and end apart: 33, of which 33 were waited for; matrix products, arithmetic and copies ran while one was open for 2% of the time, Pallas kernels for 0%

profile of v1, /device:TPU:8, one launch (start us, length us, event | category | flops | bytes accessed | tf_op | source)
XLA Modules:
  0.0 920.8 jit_solution(5920666272640544793)
XLA Ops:
  33.9 867.1 %while.19 = (s32[]{:T(128)}, bf16[32,2048]{1,0:T(8,128)(2,1)S(1)}, bf16[4,32,2048]{2,1,0:T(8,128)(2,1)}, f32[2048,32]{0,1:T(8,128)S(1)}, pred[]{:T(512)}, /*inde...) while((s32[]{:T(128)}, bf16[32,2048]{1,0:T(8,128)(2,1)S(1)}, ...), condition=%wide.region_11.12_spmd.clone, body=%wide.region_4.11_spmd.clone.sunk | while | flops 2205590528 | bytes 29810108 | solution.py:150
  41.6 23.3 %all-to-all-done = bf16[32,7,2048]{2,1,0:T(8,128)(2,1)S(1)} async-done(((bf16[32,7,2048]{2,1,0:T(8,128)(2,1)}), bf16[32,7,2048]{2,1,0:T(8,128)(2,1)S(1)}, u32[]{:S(2)}, u32[]{:S(2)}) %all-to-all-start) | async-done | bytes 917536 | tf_op jit(solution)/shard_map/while/body/eval_jaxpr/all_to_all | solution.py:112
  73.3 21.5 %all-to-all-done.1 = bf16[32,7,2048]{2,1,0:T(8,128)(2,1)S(1)} async-done(((bf16[32,7,2048]{2,1,0:T(8,128)(2,1)}), bf16[32,7,2048]{2,1,0:T(8,128)(2,1)S(1)}, u32[]{:S(2)}, u32[]{:S(2)}) %all-to-all-start.1) | async-done | bytes 917536 | tf_op jit(solution)/shard_map/while/body/eval_jaxpr/all_to_all | solution.py:115
  111.6 28.2 %all-to-all-done = bf16[32,7,2048]{2,1,0:T(8,128)(2,1)S(1)} async-done(((bf16[32,7,2048]{2,1,0:T(8,128)(2,1)}), bf16[32,7,2048]{2,1,0:T(8,128)(2,1)S(1)}, u32[]{:S(2)}, u32[]{:S(2)}) %all-to-all-start) | async-done | bytes 917536 | tf_op jit(solution)/shard_map/while/body/eval_jaxpr/all_to_all | solution.py:112
  147.6 26.8 %all-to-all-done.1 = bf16[32,7,2048]{2,1,0:T(8,128)(2,1)S(1)} async-done(((bf16[32,7,2048]{2,1,0:T(8,128)(2,1)}), bf16[32,7,2048]{2,1,0:T(8,128)(2,1)S(1)}, u32[]{:S(2)}, u32[]{:S(2)}) %all-to-all-start.1) | async-done | bytes 917536 | tf_op jit(solution)/shard_map/while/body/eval_jaxpr/all_to_all | solution.py:115
  198.3 20.5 %all-to-all-done = bf16[32,7,2048]{2,1,0:T(8,128)(2,1)S(1)} async-done(((bf16[32,7,2048]{2,1,0:T(8,128)(2,1)}), bf16[32,7,2048]{2,1,0:T(8,128)(2,1)S(1)}, u32[]{:S(2)}, u32[]{:S(2)}) %all-to-all-start) | async-done | bytes 917536 | tf_op jit(solution)/shard_map/while/body/eval_jaxpr/all_to_all | solution.py:112
  234.8 16.7 %all-to-all-done.1 = bf16[32,7,2048]{2,1,0:T(8,128)(2,1)S(1)} async-done(((bf16[32,7,2048]{2,1,0:T(8,128)(2,1)}), bf16[32,7,2048]{2,1,0:T(8,128)(2,1)S(1)}, u32[]{:S(2)}, u32[]{:S(2)}) %all-to-all-start.1) | async-done | bytes 917536 | tf_op jit(solution)/shard_map/while/body/eval_jaxpr/all_to_all | solution.py:115
  255.1 17.5 %collective-permute-done = bf16[32,2048]{1,0:T(8,128)(2,1)S(1)} collective-permute-done((bf16[32,2048]{1,0:T(8,128)(2,1)S(1)}, bf16[32,2048]{1,0:T(8,128)(2,1)S(1)}, u32[]{:S(2)}, u32[]{:S(2)}) %collective-permute-start) | collective-permute-done | bytes 131104 | tf_op jit(solution)/shard_map/while/body/eval_jaxpr/ppermute | solution.py:20
  284.4 18.1 %all-to-all-done = bf16[32,7,2048]{2,1,0:T(8,128)(2,1)S(1)} async-done(((bf16[32,7,2048]{2,1,0:T(8,128)(2,1)}), bf16[32,7,2048]{2,1,0:T(8,128)(2,1)S(1)}, u32[]{:S(2)}, u32[]{:S(2)}) %all-to-all-start) | async-done | bytes 917536 | tf_op jit(solution)/shard_map/while/body/eval_jaxpr/all_to_all | solution.py:112
  320.4 16.7 %all-to-all-done.1 = bf16[32,7,2048]{2,1,0:T(8,128)(2,1)S(1)} async-done(((bf16[32,7,2048]{2,1,0:T(8,128)(2,1)}), bf16[32,7,2048]{2,1,0:T(8,128)(2,1)S(1)}, u32[]{:S(2)}, u32[]{:S(2)}) %all-to-all-start.1) | async-done | bytes 917536 | tf_op jit(solution)/shard_map/while/body/eval_jaxpr/all_to_all | solution.py:115
  340.7 18.0 %collective-permute-done = bf16[32,2048]{1,0:T(8,128)(2,1)S(1)} collective-permute-done((bf16[32,2048]{1,0:T(8,128)(2,1)S(1)}, bf16[32,2048]{1,0:T(8,128)(2,1)S(1)}, u32[]{:S(2)}, u32[]{:S(2)}) %collective-permute-start) | collective-permute-done | bytes 131104 | tf_op jit(solution)/shard_map/while/body/eval_jaxpr/ppermute | solution.py:20
  370.4 18.1 %all-to-all-done = bf16[32,7,2048]{2,1,0:T(8,128)(2,1)S(1)} async-done(((bf16[32,7,2048]{2,1,0:T(8,128)(2,1)}), bf16[32,7,2048]{2,1,0:T(8,128)(2,1)S(1)}, u32[]{:S(2)}, u32[]{:S(2)}) %all-to-all-start) | async-done | bytes 917536 | tf_op jit(solution)/shard_map/while/body/eval_jaxpr/all_to_all | solution.py:112
  406.5 16.7 %all-to-all-done.1 = bf16[32,7,2048]{2,1,0:T(8,128)(2,1)S(1)} async-done(((bf16[32,7,2048]{2,1,0:T(8,128)(2,1)}), bf16[32,7,2048]{2,1,0:T(8,128)(2,1)S(1)}, u32[]{:S(2)}, u32[]{:S(2)}) %all-to-all-start.1) | async-done | bytes 917536 | tf_op jit(solution)/shard_map/while/body/eval_jaxpr/all_to_all | solution.py:115
  449.3 17.5 %all-to-all-done = bf16[32,7,2048]{2,1,0:T(8,128)(2,1)S(1)} async-done(((bf16[32,7,2048]{2,1,0:T(8,128)(2,1)}), bf16[32,7,2048]{2,1,0:T(8,128)(2,1)S(1)}, u32[]{:S(2)}, u32[]{:S(2)}) %all-to-all-start) | async-done | bytes 917536 | tf_op jit(solution)/shard_map/while/body/eval_jaxpr/all_to_all | solution.py:112
  484.9 16.7 %all-to-all-done.1 = bf16[32,7,2048]{2,1,0:T(8,128)(2,1)S(1)} async-done(((bf16[32,7,2048]{2,1,0:T(8,128)(2,1)}), bf16[32,7,2048]{2,1,0:T(8,128)(2,1)S(1)}, u32[]{:S(2)}, u32[]{:S(2)}) %all-to-all-start.1) | async-done | bytes 917536 | tf_op jit(solution)/shard_map/while/body/eval_jaxpr/all_to_all | solution.py:115
  526.6 17.8 %all-to-all-done = bf16[32,7,2048]{2,1,0:T(8,128)(2,1)S(1)} async-done(((bf16[32,7,2048]{2,1,0:T(8,128)(2,1)}), bf16[32,7,2048]{2,1,0:T(8,128)(2,1)S(1)}, u32[]{:S(2)}, u32[]{:S(2)}) %all-to-all-start) | async-done | bytes 917536 | tf_op jit(solution)/shard_map/while/body/eval_jaxpr/all_to_all | solution.py:112
  553.3 24.1 %all-to-all-done.1 = bf16[32,7,2048]{2,1,0:T(8,128)(2,1)S(1)} async-done(((bf16[32,7,2048]{2,1,0:T(8,128)(2,1)}), bf16[32,7,2048]{2,1,0:T(8,128)(2,1)S(1)}, u32[]{:S(2)}, u32[]{:S(2)}) %all-to-all-start.1) | async-done | bytes 917536 | tf_op jit(solution)/shard_map/while/body/eval_jaxpr/all_to_all | solution.py:115
  603.8 18.1 %all-to-all-done = bf16[32,7,2048]{2,1,0:T(8,128)(2,1)S(1)} async-done(((bf16[32,7,2048]{2,1,0:T(8,128)(2,1)}), bf16[32,7,2048]{2,1,0:T(8,128)(2,1)S(1)}, u32[]{:S(2)}, u32[]{:S(2)}) %all-to-all-start) | async-done | bytes 917536 | tf_op jit(solution)/shard_map/while/body/eval_jaxpr/all_to_all | solution.py:112
  681.0 20.6 %all-to-all-done = bf16[32,7,2048]{2,1,0:T(8,128)(2,1)S(1)} async-done(((bf16[32,7,2048]{2,1,0:T(8,128)(2,1)}), bf16[32,7,2048]{2,1,0:T(8,128)(2,1)S(1)}, u32[]{:S(2)}, u32[]{:S(2)}) %all-to-all-start) | async-done | bytes 917536 | tf_op jit(solution)/shard_map/while/body/eval_jaxpr/all_to_all | solution.py:112
  758.3 18.1 %all-to-all-done = bf16[32,7,2048]{2,1,0:T(8,128)(2,1)S(1)} async-done(((bf16[32,7,2048]{2,1,0:T(8,128)(2,1)}), bf16[32,7,2048]{2,1,0:T(8,128)(2,1)S(1)}, u32[]{:S(2)}, u32[]{:S(2)}) %all-to-all-start) | async-done | bytes 917536 | tf_op jit(solution)/shard_map/while/body/eval_jaxpr/all_to_all | solution.py:112
  787.4 16.7 %all-to-all-done.1 = bf16[32,7,2048]{2,1,0:T(8,128)(2,1)S(1)} async-done(((bf16[32,7,2048]{2,1,0:T(8,128)(2,1)}), bf16[32,7,2048]{2,1,0:T(8,128)(2,1)S(1)}, u32[]{:S(2)}, u32[]{:S(2)}) %all-to-all-start.1) | async-done | bytes 917536 | tf_op jit(solution)/shard_map/while/body/eval_jaxpr/all_to_all | solution.py:115
  835.5 20.9 %all-to-all-done = bf16[32,7,2048]{2,1,0:T(8,128)(2,1)S(1)} async-done(((bf16[32,7,2048]{2,1,0:T(8,128)(2,1)}), bf16[32,7,2048]{2,1,0:T(8,128)(2,1)S(1)}, u32[]{:S(2)}, u32[]{:S(2)}) %all-to-all-start) | async-done | bytes 917536 | tf_op jit(solution)/shard_map/while/body/eval_jaxpr/all_to_all | solution.py:112
  869.1 16.7 %all-to-all-done.1 = bf16[32,7,2048]{2,1,0:T(8,128)(2,1)S(1)} async-done(((bf16[32,7,2048]{2,1,0:T(8,128)(2,1)}), bf16[32,7,2048]{2,1,0:T(8,128)(2,1)S(1)}, u32[]{:S(2)}, u32[]{:S(2)}) %all-to-all-start.1) | async-done | bytes 917536 | tf_op jit(solution)/shard_map/while/body/eval_jaxpr/all_to_all | solution.py:115
  901.5 18.4 %all_to_all.29 = bf16[32,2,1024]{2,1,0:T(2,128)(2,1)S(1)} all-to-all(bf16[32,2,1024]{2,1,0:T(2,128)(2,1)S(1)} %reshape.72), channel_id=1, replica_groups=mesh['section'=8,'dp_0'=4,'dp_1'=8] {'dp_0','dp_1'}, dimensions={0} | all-to-all | bytes 262144 | tf_op jit(solution)/shard_map/all_to_all | solution.py:31
  (309 shorter events, 506.4 us)
Async XLA Ops:
  37.4 27.5 %all-to-all-start = ((bf16[32,7,2048]{2,1,0:T(8,128)(2,1)}), bf16[32,7,2048]{2,1,0:T(8,128)(2,1)S(1)}, u32[]{:S(2)}, u32[]{:S(2)}) async-start(bf16[32,7,2048]{2,1,0:T(8,128)(2,1)} %copy.69), calls=%async_computation | async-start | bytes 2097152 | tf_op jit(solution)/shard_map/while/body/eval_jaxpr/all_to_all | solution.py:112
  66.3 28.5 %all-to-all-start.1 = ((bf16[32,7,2048]{2,1,0:T(8,128)(2,1)}), bf16[32,7,2048]{2,1,0:T(8,128)(2,1)S(1)}, u32[]{:S(2)}, u32[]{:S(2)}) async-start(bf16[32,7,2048]{2,1,0:T(8,128)(2,1)} %reshape.75), calls=%async_computation.1 | async-start | bytes 2097152 | tf_op jit(solution)/shard_map/while/body/eval_jaxpr/all_to_all | solution.py:115
  105.9 33.9 %all-to-all-start = ((bf16[32,7,2048]{2,1,0:T(8,128)(2,1)}), bf16[32,7,2048]{2,1,0:T(8,128)(2,1)S(1)}, u32[]{:S(2)}, u32[]{:S(2)}) async-start(bf16[32,7,2048]{2,1,0:T(8,128)(2,1)} %copy.69), calls=%async_computation | async-start | bytes 2097152 | tf_op jit(solution)/shard_map/while/body/eval_jaxpr/all_to_all | solution.py:112
  141.2 33.2 %all-to-all-start.1 = ((bf16[32,7,2048]{2,1,0:T(8,128)(2,1)}), bf16[32,7,2048]{2,1,0:T(8,128)(2,1)S(1)}, u32[]{:S(2)}, u32[]{:S(2)}) async-start(bf16[32,7,2048]{2,1,0:T(8,128)(2,1)} %reshape.75), calls=%async_computation.1 | async-start | bytes 2097152 | tf_op jit(solution)/shard_map/while/body/eval_jaxpr/all_to_all | solution.py:115
  189.6 29.2 %all-to-all-start = ((bf16[32,7,2048]{2,1,0:T(8,128)(2,1)}), bf16[32,7,2048]{2,1,0:T(8,128)(2,1)S(1)}, u32[]{:S(2)}, u32[]{:S(2)}) async-start(bf16[32,7,2048]{2,1,0:T(8,128)(2,1)} %copy.69), calls=%async_computation | async-start | bytes 2097152 | tf_op jit(solution)/shard_map/while/body/eval_jaxpr/all_to_all | solution.py:112
  229.0 22.4 %all-to-all-start.1 = ((bf16[32,7,2048]{2,1,0:T(8,128)(2,1)}), bf16[32,7,2048]{2,1,0:T(8,128)(2,1)S(1)}, u32[]{:S(2)}, u32[]{:S(2)}) async-start(bf16[32,7,2048]{2,1,0:T(8,128)(2,1)} %reshape.75), calls=%async_computation.1 | async-start | bytes 2097152 | tf_op jit(solution)/shard_map/while/body/eval_jaxpr/all_to_all | solution.py:115
  252.8 19.8 %collective-permute-start = (bf16[32,2048]{1,0:T(8,128)(2,1)S(1)}, bf16[32,2048]{1,0:T(8,128)(2,1)S(1)}, u32[]{:S(2)}, u32[]{:S(2)}) collective-permute-start(bf16[32,2048]{1,0:T(8,128)(2,1)S(1)} %get-tuple-element.542), channel_id=1, source_target_pairs={{0,32},{32,64},{64,96},{96,128},{128,160},{160,192},{192,224},{1,3... | collective-permute-start | bytes 393224 | tf_op jit(solution)/shard_map/while/body/eval_jaxpr/ppermute | solution.py:20
  276.1 26.4 %all-to-all-start = ((bf16[32,7,2048]{2,1,0:T(8,128)(2,1)}), bf16[32,7,2048]{2,1,0:T(8,128)(2,1)S(1)}, u32[]{:S(2)}, u32[]{:S(2)}) async-start(bf16[32,7,2048]{2,1,0:T(8,128)(2,1)} %copy.69), calls=%async_computation | async-start | bytes 2097152 | tf_op jit(solution)/shard_map/while/body/eval_jaxpr/all_to_all | solution.py:112
  312.7 24.4 %all-to-all-start.1 = ((bf16[32,7,2048]{2,1,0:T(8,128)(2,1)}), bf16[32,7,2048]{2,1,0:T(8,128)(2,1)S(1)}, u32[]{:S(2)}, u32[]{:S(2)}) async-start(bf16[32,7,2048]{2,1,0:T(8,128)(2,1)} %reshape.75), calls=%async_computation.1 | async-start | bytes 2097152 | tf_op jit(solution)/shard_map/while/body/eval_jaxpr/all_to_all | solution.py:115
  338.4 20.2 %collective-permute-start = (bf16[32,2048]{1,0:T(8,128)(2,1)S(1)}, bf16[32,2048]{1,0:T(8,128)(2,1)S(1)}, u32[]{:S(2)}, u32[]{:S(2)}) collective-permute-start(bf16[32,2048]{1,0:T(8,128)(2,1)S(1)} %get-tuple-element.542), channel_id=1, source_target_pairs={{0,32},{32,64},{64,96},{96,128},{128,160},{160,192},{192,224},{1,3... | collective-permute-start | bytes 393224 | tf_op jit(solution)/shard_map/while/body/eval_jaxpr/ppermute | solution.py:20
  362.1 26.4 %all-to-all-start = ((bf16[32,7,2048]{2,1,0:T(8,128)(2,1)}), bf16[32,7,2048]{2,1,0:T(8,128)(2,1)S(1)}, u32[]{:S(2)}, u32[]{:S(2)}) async-start(bf16[32,7,2048]{2,1,0:T(8,128)(2,1)} %copy.69), calls=%async_computation | async-start | bytes 2097152 | tf_op jit(solution)/shard_map/while/body/eval_jaxpr/all_to_all | solution.py:112
  398.8 24.4 %all-to-all-start.1 = ((bf16[32,7,2048]{2,1,0:T(8,128)(2,1)}), bf16[32,7,2048]{2,1,0:T(8,128)(2,1)S(1)}, u32[]{:S(2)}, u32[]{:S(2)}) async-start(bf16[32,7,2048]{2,1,0:T(8,128)(2,1)} %reshape.75), calls=%async_computation.1 | async-start | bytes 2097152 | tf_op jit(solution)/shard_map/while/body/eval_jaxpr/all_to_all | solution.py:115
  443.4 23.4 %all-to-all-start = ((bf16[32,7,2048]{2,1,0:T(8,128)(2,1)}), bf16[32,7,2048]{2,1,0:T(8,128)(2,1)S(1)}, u32[]{:S(2)}, u32[]{:S(2)}) async-start(bf16[32,7,2048]{2,1,0:T(8,128)(2,1)} %copy.69), calls=%async_computation | async-start | bytes 2097152 | tf_op jit(solution)/shard_map/while/body/eval_jaxpr/all_to_all | solution.py:112
  477.0 24.5 %all-to-all-start.1 = ((bf16[32,7,2048]{2,1,0:T(8,128)(2,1)}), bf16[32,7,2048]{2,1,0:T(8,128)(2,1)S(1)}, u32[]{:S(2)}, u32[]{:S(2)}) async-start(bf16[32,7,2048]{2,1,0:T(8,128)(2,1)} %reshape.75), calls=%async_computation.1 | async-start | bytes 2097152 | tf_op jit(solution)/shard_map/while/body/eval_jaxpr/all_to_all | solution.py:115
  518.3 26.1 %all-to-all-start = ((bf16[32,7,2048]{2,1,0:T(8,128)(2,1)}), bf16[32,7,2048]{2,1,0:T(8,128)(2,1)S(1)}, u32[]{:S(2)}, u32[]{:S(2)}) async-start(bf16[32,7,2048]{2,1,0:T(8,128)(2,1)} %copy.69), calls=%async_computation | async-start | bytes 2097152 | tf_op jit(solution)/shard_map/while/body/eval_jaxpr/all_to_all | solution.py:112
  545.8 31.7 %all-to-all-start.1 = ((bf16[32,7,2048]{2,1,0:T(8,128)(2,1)}), bf16[32,7,2048]{2,1,0:T(8,128)(2,1)S(1)}, u32[]{:S(2)}, u32[]{:S(2)}) async-start(bf16[32,7,2048]{2,1,0:T(8,128)(2,1)} %reshape.75), calls=%async_computation.1 | async-start | bytes 2097152 | tf_op jit(solution)/shard_map/while/body/eval_jaxpr/all_to_all | solution.py:115
  595.5 26.4 %all-to-all-start = ((bf16[32,7,2048]{2,1,0:T(8,128)(2,1)}), bf16[32,7,2048]{2,1,0:T(8,128)(2,1)S(1)}, u32[]{:S(2)}, u32[]{:S(2)}) async-start(bf16[32,7,2048]{2,1,0:T(8,128)(2,1)} %copy.69), calls=%async_computation | async-start | bytes 2097152 | tf_op jit(solution)/shard_map/while/body/eval_jaxpr/all_to_all | solution.py:112
  623.3 26.5 %all-to-all-start.1 = ((bf16[32,7,2048]{2,1,0:T(8,128)(2,1)}), bf16[32,7,2048]{2,1,0:T(8,128)(2,1)S(1)}, u32[]{:S(2)}, u32[]{:S(2)}) async-start(bf16[32,7,2048]{2,1,0:T(8,128)(2,1)} %reshape.75), calls=%async_computation.1 | async-start | bytes 2097152 | tf_op jit(solution)/shard_map/while/body/eval_jaxpr/all_to_all | solution.py:115
  672.7 28.9 %all-to-all-start = ((bf16[32,7,2048]{2,1,0:T(8,128)(2,1)}), bf16[32,7,2048]{2,1,0:T(8,128)(2,1)S(1)}, u32[]{:S(2)}, u32[]{:S(2)}) async-start(bf16[32,7,2048]{2,1,0:T(8,128)(2,1)} %copy.69), calls=%async_computation | async-start | bytes 2097152 | tf_op jit(solution)/shard_map/while/body/eval_jaxpr/all_to_all | solution.py:112
  703.0 28.3 %all-to-all-start.1 = ((bf16[32,7,2048]{2,1,0:T(8,128)(2,1)}), bf16[32,7,2048]{2,1,0:T(8,128)(2,1)S(1)}, u32[]{:S(2)}, u32[]{:S(2)}) async-start(bf16[32,7,2048]{2,1,0:T(8,128)(2,1)} %reshape.75), calls=%async_computation.1 | async-start | bytes 2097152 | tf_op jit(solution)/shard_map/while/body/eval_jaxpr/all_to_all | solution.py:115
  750.0 26.4 %all-to-all-start = ((bf16[32,7,2048]{2,1,0:T(8,128)(2,1)}), bf16[32,7,2048]{2,1,0:T(8,128)(2,1)S(1)}, u32[]{:S(2)}, u32[]{:S(2)}) async-start(bf16[32,7,2048]{2,1,0:T(8,128)(2,1)} %copy.69), calls=%async_computation | async-start | bytes 2097152 | tf_op jit(solution)/shard_map/while/body/eval_jaxpr/all_to_all | solution.py:112
  777.8 26.3 %all-to-all-start.1 = ((bf16[32,7,2048]{2,1,0:T(8,128)(2,1)}), bf16[32,7,2048]{2,1,0:T(8,128)(2,1)S(1)}, u32[]{:S(2)}, u32[]{:S(2)}) async-start(bf16[32,7,2048]{2,1,0:T(8,128)(2,1)} %reshape.75), calls=%async_computation.1 | async-start | bytes 2097152 | tf_op jit(solution)/shard_map/while/body/eval_jaxpr/all_to_all | solution.py:115
  827.2 29.2 %all-to-all-start = ((bf16[32,7,2048]{2,1,0:T(8,128)(2,1)}), bf16[32,7,2048]{2,1,0:T(8,128)(2,1)S(1)}, u32[]{:S(2)}, u32[]{:S(2)}) async-start(bf16[32,7,2048]{2,1,0:T(8,128)(2,1)} %copy.69), calls=%async_computation | async-start | bytes 2097152 | tf_op jit(solution)/shard_map/while/body/eval_jaxpr/all_to_all | solution.py:112
  857.8 27.9 %all-to-all-start.1 = ((bf16[32,7,2048]{2,1,0:T(8,128)(2,1)}), bf16[32,7,2048]{2,1,0:T(8,128)(2,1)S(1)}, u32[]{:S(2)}, u32[]{:S(2)}) async-start(bf16[32,7,2048]{2,1,0:T(8,128)(2,1)} %reshape.75), calls=%async_computation.1 | async-start | bytes 2097152 | tf_op jit(solution)/shard_map/while/body/eval_jaxpr/all_to_all | solution.py:115
  (9 other events, 121.0 us)
